TPU v7x, 256 devices: a whole 4x4x8 slice. The times are simulated.
256 devices in a mesh: span: 16 (over y, z_lo, core), seq: 16 (over z_hi, x).
Axes of the slice: x: 4, y: 4, z: 8 (z_hi: 4, z_lo: 2; z = z_hi * 2 + z_lo), core: 2. Of those that a mesh axis runs over, the one named last changes fastest.
Arguments:
- query: bfloat16 [16, 2048, 48, 128], P('span', 'seq'), may hold values from -8 to 8
- keys: bfloat16 [16, 2048, 48, 128], P('span', 'seq'), may hold values from -6 to 6
- values: bfloat16 [16, 2048, 48, 128], P('span', 'seq'), may hold values from -6 to 6
- block_list: int32 [16, 16, 32], P('span'), may hold values from 0 to 31, as said below
- block_count: int32 [16, 16], P('span'), may hold values from 1 to 32
Outputs:
- attended: bfloat16 [16, 2048, 48, 128], P('span', 'seq')
Inputs may be any that keep to these rules, and one draw needn't show every extreme that they name: `block_list`: each row names every one of the 32 tiles once; the used slots of query tile t name exactly the own tiles 16 to 16 + t and, for spans after the first, some of the previous span's tiles (none for span 0); slots at or after block_count are not used.
All inputs are finite; a program needn't handle non-finite values.
Results may differ from a plain program's by a relative error of at most 0.005.
Values may be sent and summed in bfloat16 or wider, within the bound.
A program may use at most 128 MiB of HBM per device.

v0:
```python
import math

import jax
import jax.numpy as jnp
from jax import lax
from jax.sharding import PartitionSpec as P


def shifted(value, axis, steps):
    count = lax.axis_size(axis)
    leading, last = (max(0, -steps), min(count, count - steps))
    return lax.ppermute(value, axis, [(source, source + steps) for source in range(leading, last)])


def visible_tiles(tile_lists, tile_counts):
    pool_count = tile_lists.shape[1]
    slots = jnp.arange(pool_count, dtype=jnp.int32)
    used = slots[None, :] < tile_counts[:, None]
    named = (tile_lists[:, :, None] == slots[None, None, :]) & used[:, :, None]
    return jnp.any(named, axis=1)


def attend(query, keys, values, earlier_keys, earlier_values, seen):
    tile_count = seen.shape[0]
    tile_rows = query.shape[0] // tile_count
    head_count = query.shape[1]
    head_width = query.shape[2]
    pool_keys = jnp.concatenate([earlier_keys, keys], 0)
    pool_values = jnp.concatenate([earlier_values, values], 0)
    key_tile = jnp.arange(2 * tile_count * tile_rows, dtype=jnp.int32) // tile_rows
    score_scale = 1.0 / math.sqrt(head_width)
    per_block = math.gcd(tile_count, max(1, 256 // tile_rows))
    blocks = tile_count // per_block
    query_blocks = query.reshape(blocks, per_block, tile_rows, head_count, head_width)
    seen_blocks = seen.reshape(blocks, per_block, 2 * tile_count)

    def one_block(item):
        query_block, seen_block = item
        scores = (
            jnp.einsum("gqhd,khd->ghqk", query_block, pool_keys, preferred_element_type=jnp.float32)
            * score_scale
        )
        visible = seen_block[:, key_tile][:, None, None, :]
        masked = jnp.where(visible, scores, -jnp.inf)
        largest = jnp.max(masked, axis=-1, keepdims=True)
        weights = jnp.where(visible, jnp.exp(masked - largest), 0.0)
        summed = jnp.sum(weights, axis=-1, keepdims=True)
        weights_bf = (weights / summed).astype(jnp.bfloat16)
        result = jnp.einsum(
            "ghqk,khd->gqhd", weights_bf, pool_values, preferred_element_type=jnp.float32
        )
        return result.astype(jnp.bfloat16)

    return lax.map(one_block, (query_blocks, seen_blocks)).reshape(query.shape)


def grouped(array, group_count):
    return array.reshape(
        1, array.shape[1], group_count, array.shape[2] // group_count, array.shape[3]
    )


def per_device(query, keys, values, block_list, block_count):
    seen = visible_tiles(block_list[0], block_count[0])
    group_count = lax.axis_size("seq")
    query_g = grouped(query, group_count)
    keys_g = grouped(keys, group_count)
    values_g = grouped(values, group_count)
    earlier_keys, earlier_values = shifted((keys_g, values_g), "span", 1)
    query_part = lax.all_to_all(query_g, "seq", split_axis=2, concat_axis=1, tiled=True)
    keys_part = lax.all_to_all(keys_g, "seq", split_axis=2, concat_axis=1, tiled=True)
    values_part = lax.all_to_all(values_g, "seq", split_axis=2, concat_axis=1, tiled=True)
    earlier_kpart = lax.all_to_all(earlier_keys, "seq", split_axis=2, concat_axis=1, tiled=True)
    earlier_vpart = lax.all_to_all(earlier_values, "seq", split_axis=2, concat_axis=1, tiled=True)
    gathered = attend(
        query_part[0, :, 0],
        keys_part[0, :, 0],
        values_part[0, :, 0],
        earlier_kpart[0, :, 0],
        earlier_vpart[0, :, 0],
        seen,
    )[None, :, None]
    returned = lax.all_to_all(gathered, "seq", split_axis=1, concat_axis=2, tiled=True)
    return returned.reshape(query.shape)


def solution(mesh):
    in_specs = (
        P("span", "seq", None, None),
        P("span", "seq", None, None),
        P("span", "seq", None, None),
        P("span", None, None),
        P("span", None),
    )
    out_specs = P("span", "seq", None, None)
    return jax.shard_map(
        per_device, mesh=mesh, in_specs=in_specs, out_specs=out_specs, check_vma=False
    )
```

profile of v0, /device:TPU:11, one launch (start us, length us, event | category | flops | bytes accessed | tf_op | source)
XLA Modules:
  0.0 663.2 jit_solution(5535153775909613295)
XLA Ops:
  3.1 10.9 %all-to-all-start.2 = ((bf16[1,128,16,3,128]{4,1,3,0,2:T(8,128)(2,1)}), bf16[1,128,16,3,128]{4,1,3,0,2:T(8,128)(2,1)S(1)}, u32[]{:S(2)}, u32[]{:S(2)}) async-start(bf16[1,128,16,3,128]{4,1,3,0,2:T(8,128)(2,1)} %bitcast.12), calls=%async_computation.2 | async-start | bytes 3145728 | tf_op jit(solution)/shard_map/all_to_all | solution.py:71
  15.6 33.2 %all-to-all-done.2 = bf16[1,128,16,3,128]{4,1,3,0,2:T(8,128)(2,1)S(1)} async-done(((bf16[1,128,16,3,128]{4,1,3,0,2:T(8,128)(2,1)}), bf16[1,128,16,3,128]{4,1,3,0,2:T(8,128)(2,1)S(1)}, u32[]{:S(2)}, u32[]{:S(2)}) %all-to-all-start.2) | async-done | bytes 1572896 | tf_op jit(solution)/shard_map/all_to_all | solution.py:71
  62.8 47.4 %collective-permute-done = bf16[1,128,16,3,128]{4,1,3,2,0:T(8,128)(2,1)} collective-permute-done((bf16[1,128,16,3,128]{4,1,3,2,0:T(8,128)(2,1)}, bf16[1,128,16,3,128]{4,1,3,2,0:T(8,128)(2,1)}, u32[]{:S(2)}, u32[]{:S(2)}) %collective-permute-start) | collective-permute-done | bytes 1572896 | tf_op jit(solution)/shard_map/ppermute | solution.py:12
  123.3 46.5 %collective-permute-done.1 = bf16[1,128,16,3,128]{4,1,3,2,0:T(8,128)(2,1)} collective-permute-done((bf16[1,128,16,3,128]{4,1,3,2,0:T(8,128)(2,1)}, bf16[1,128,16,3,128]{4,1,3,2,0:T(8,128)(2,1)}, u32[]{:S(2)}, u32[]{:S(2)}) %collective-permute-start.1) | collective-permute-done | bytes 1572896 | tf_op jit(solution)/shard_map/ppermute | solution.py:12
  181.6 32.8 %all-to-all-done.3 = bf16[1,128,16,3,128]{4,1,3,0,2:T(8,128)(2,1)} async-done(((bf16[1,128,16,3,128]{4,1,3,0,2:T(8,128)(2,1)}), bf16[1,128,16,3,128]{4,1,3,0,2:T(8,128)(2,1)}, u32[]{:S(2)}, u32[]{:S(2)}) %all-to-all-start.3) | async-done | bytes 1572896 | tf_op jit(solution)/shard_map/all_to_all | solution.py:74
  232.9 24.3 %all-to-all-done = bf16[1,128,16,3,128]{4,1,3,0,2:T(8,128)(2,1)} async-done(((bf16[1,128,16,3,128]{4,1,3,0,2:T(8,128)(2,1)}), bf16[1,128,16,3,128]{4,1,3,0,2:T(8,128)(2,1)}, u32[]{:S(2)}, u32[]{:S(2)}) %all-to-all-start) | async-done | bytes 1572896 | tf_op jit(solution)/shard_map/all_to_all | solution.py:70
  257.2 356.4 %while.11 = (s32[]{:T(128)}, bf16[8,2,128,3,128]{4,2,1,0,3:T(8,128)(2,1)}, pred[8,2,32]{2,1,0:T(4,128)(4,1)S(1)}, bf16[8,2,128,3,128]{4,2,3,1,0:T(8,128)(2,1)}, ...) while((s32[]{:T(128)}, ...), condition=%wide.region_4.5_spmd.clone, body=%wide.region_1.4_spmd.clone.sunk | while | flops 1639075840 | bytes 69746032 | solution.py:54
  264.7 14.6 %gather_fusion = pred[4096,2]{1,0:T(8,128)(4,1)} fusion(pred[2,32]{0,1:T(8,128)(4,1)S(1)} %copy.90, s32[4096]{0:T(1024)S(1)} %broadcast_clamp_fusion.2), kind=kCustom, calls=%fused_computation.clone.clone.1 | custom fusion | bytes 32768 | tf_op jit(solution)/shard_map/while/body/eval_jaxpr/gather | solution.py:43
  280.9 13.7 %fusion.40 = (f32[2,3,128]{2,0,1:T(2,128)S(1)}, f32[2,3,128,4096]{3,2,0,1:T(8,128)}) fusion(f32[3,2,128,4096]{3,2,1,0:T(8,128)} %fusion.39, pred[2,4096]{1,0:T(4,128)(4,1)S(1)} %copy.91), kind=kOutput, calls=%fused_computation.40.clone.1 | output fusion | flops 22024192 | bytes 25177088 | tf_op jit(solution)/shard_map/while/body/eval_jaxpr/sub | solution.py:46
  309.2 14.6 %gather_fusion = pred[4096,2]{1,0:T(8,128)(4,1)} fusion(pred[2,32]{0,1:T(8,128)(4,1)S(1)} %copy.90, s32[4096]{0:T(1024)S(1)} %broadcast_clamp_fusion.2), kind=kCustom, calls=%fused_computation.clone.clone.1 | custom fusion | bytes 32768 | tf_op jit(solution)/shard_map/while/body/eval_jaxpr/gather | solution.py:43
  325.4 13.7 %fusion.40 = (f32[2,3,128]{2,0,1:T(2,128)S(1)}, f32[2,3,128,4096]{3,2,0,1:T(8,128)}) fusion(f32[3,2,128,4096]{3,2,1,0:T(8,128)} %fusion.39, pred[2,4096]{1,0:T(4,128)(4,1)S(1)} %copy.91), kind=kOutput, calls=%fused_computation.40.clone.1 | output fusion | flops 22024192 | bytes 25177088 | tf_op jit(solution)/shard_map/while/body/eval_jaxpr/sub | solution.py:46
  353.8 14.6 %gather_fusion = pred[4096,2]{1,0:T(8,128)(4,1)} fusion(pred[2,32]{0,1:T(8,128)(4,1)S(1)} %copy.90, s32[4096]{0:T(1024)S(1)} %broadcast_clamp_fusion.2), kind=kCustom, calls=%fused_computation.clone.clone.1 | custom fusion | bytes 32768 | tf_op jit(solution)/shard_map/while/body/eval_jaxpr/gather | solution.py:43
  370.0 13.7 %fusion.40 = (f32[2,3,128]{2,0,1:T(2,128)S(1)}, f32[2,3,128,4096]{3,2,0,1:T(8,128)}) fusion(f32[3,2,128,4096]{3,2,1,0:T(8,128)} %fusion.39, pred[2,4096]{1,0:T(4,128)(4,1)S(1)} %copy.91), kind=kOutput, calls=%fused_computation.40.clone.1 | output fusion | flops 22024192 | bytes 25177088 | tf_op jit(solution)/shard_map/while/body/eval_jaxpr/sub | solution.py:46
  398.3 14.6 %gather_fusion = pred[4096,2]{1,0:T(8,128)(4,1)} fusion(pred[2,32]{0,1:T(8,128)(4,1)S(1)} %copy.90, s32[4096]{0:T(1024)S(1)} %broadcast_clamp_fusion.2), kind=kCustom, calls=%fused_computation.clone.clone.1 | custom fusion | bytes 32768 | tf_op jit(solution)/shard_map/while/body/eval_jaxpr/gather | solution.py:43
  414.5 13.7 %fusion.40 = (f32[2,3,128]{2,0,1:T(2,128)S(1)}, f32[2,3,128,4096]{3,2,0,1:T(8,128)}) fusion(f32[3,2,128,4096]{3,2,1,0:T(8,128)} %fusion.39, pred[2,4096]{1,0:T(4,128)(4,1)S(1)} %copy.91), kind=kOutput, calls=%fused_computation.40.clone.1 | output fusion | flops 22024192 | bytes 25177088 | tf_op jit(solution)/shard_map/while/body/eval_jaxpr/sub | solution.py:46
  442.8 14.6 %gather_fusion = pred[4096,2]{1,0:T(8,128)(4,1)} fusion(pred[2,32]{0,1:T(8,128)(4,1)S(1)} %copy.90, s32[4096]{0:T(1024)S(1)} %broadcast_clamp_fusion.2), kind=kCustom, calls=%fused_computation.clone.clone.1 | custom fusion | bytes 32768 | tf_op jit(solution)/shard_map/while/body/eval_jaxpr/gather | solution.py:43
  459.1 13.7 %fusion.40 = (f32[2,3,128]{2,0,1:T(2,128)S(1)}, f32[2,3,128,4096]{3,2,0,1:T(8,128)}) fusion(f32[3,2,128,4096]{3,2,1,0:T(8,128)} %fusion.39, pred[2,4096]{1,0:T(4,128)(4,1)S(1)} %copy.91), kind=kOutput, calls=%fused_computation.40.clone.1 | output fusion | flops 22024192 | bytes 25177088 | tf_op jit(solution)/shard_map/while/body/eval_jaxpr/sub | solution.py:46
  487.4 14.6 %gather_fusion = pred[4096,2]{1,0:T(8,128)(4,1)} fusion(pred[2,32]{0,1:T(8,128)(4,1)S(1)} %copy.90, s32[4096]{0:T(1024)S(1)} %broadcast_clamp_fusion.2), kind=kCustom, calls=%fused_computation.clone.clone.1 | custom fusion | bytes 32768 | tf_op jit(solution)/shard_map/while/body/eval_jaxpr/gather | solution.py:43
  503.6 13.7 %fusion.40 = (f32[2,3,128]{2,0,1:T(2,128)S(1)}, f32[2,3,128,4096]{3,2,0,1:T(8,128)}) fusion(f32[3,2,128,4096]{3,2,1,0:T(8,128)} %fusion.39, pred[2,4096]{1,0:T(4,128)(4,1)S(1)} %copy.91), kind=kOutput, calls=%fused_computation.40.clone.1 | output fusion | flops 22024192 | bytes 25177088 | tf_op jit(solution)/shard_map/while/body/eval_jaxpr/sub | solution.py:46
  531.9 14.6 %gather_fusion = pred[4096,2]{1,0:T(8,128)(4,1)} fusion(pred[2,32]{0,1:T(8,128)(4,1)S(1)} %copy.90, s32[4096]{0:T(1024)S(1)} %broadcast_clamp_fusion.2), kind=kCustom, calls=%fused_computation.clone.clone.1 | custom fusion | bytes 32768 | tf_op jit(solution)/shard_map/while/body/eval_jaxpr/gather | solution.py:43
  548.2 13.7 %fusion.40 = (f32[2,3,128]{2,0,1:T(2,128)S(1)}, f32[2,3,128,4096]{3,2,0,1:T(8,128)}) fusion(f32[3,2,128,4096]{3,2,1,0:T(8,128)} %fusion.39, pred[2,4096]{1,0:T(4,128)(4,1)S(1)} %copy.91), kind=kOutput, calls=%fused_computation.40.clone.1 | output fusion | flops 22024192 | bytes 25177088 | tf_op jit(solution)/shard_map/while/body/eval_jaxpr/sub | solution.py:46
  576.5 14.6 %gather_fusion = pred[4096,2]{1,0:T(8,128)(4,1)} fusion(pred[2,32]{0,1:T(8,128)(4,1)S(1)} %copy.90, s32[4096]{0:T(1024)S(1)} %broadcast_clamp_fusion.2), kind=kCustom, calls=%fused_computation.clone.clone.1 | custom fusion | bytes 32768 | tf_op jit(solution)/shard_map/while/body/eval_jaxpr/gather | solution.py:43
  592.7 13.7 %fusion.40 = (f32[2,3,128]{2,0,1:T(2,128)S(1)}, f32[2,3,128,4096]{3,2,0,1:T(8,128)}) fusion(f32[3,2,128,4096]{3,2,1,0:T(8,128)} %fusion.39, pred[2,4096]{1,0:T(4,128)(4,1)S(1)} %copy.91), kind=kOutput, calls=%fused_computation.40.clone.1 | output fusion | flops 22024192 | bytes 25177088 | tf_op jit(solution)/shard_map/while/body/eval_jaxpr/sub | solution.py:46
  616.8 43.9 %all_to_all.90 = bf16[1,2048,1,3,128]{4,3,2,0,1:T(4,128)(2,1)S(1)} all-to-all(bf16[1,2048,1,3,128]{4,3,2,0,1:T(4,128)(2,1)S(1)} %copy.75), channel_id=1, replica_groups=mesh['span'=16,'seq'=16] {'seq'}, dimensions={1} | all-to-all | bytes 3145728 | tf_op jit(solution)/shard_map/all_to_all | solution.py:83
  (110 shorter events, 198.2 us)
Async XLA Ops:
  0.0 14.0 %copy-start.1 = (bf16[1,128,48,128]{3,2,1,0:T(8,128)(2,1)S(1)}, bf16[1,128,48,128]{3,2,1,0:T(8,128)(2,1)}, u32[]{:S(2)}) copy-start(bf16[1,128,48,128]{3,2,1,0:T(8,128)(2,1)} %param.9) | copy-start | bytes 4718596
  3.1 45.7 %all-to-all-start.2 = ((bf16[1,128,16,3,128]{4,1,3,0,2:T(8,128)(2,1)}), bf16[1,128,16,3,128]{4,1,3,0,2:T(8,128)(2,1)S(1)}, u32[]{:S(2)}, u32[]{:S(2)}) async-start(bf16[1,128,16,3,128]{4,1,3,0,2:T(8,128)(2,1)} %bitcast.12), calls=%async_computation.2 | async-start | bytes 3145728 | tf_op jit(solution)/shard_map/all_to_all | solution.py:71
  48.7 61.4 %all-to-all-start.4 = ((bf16[1,128,16,3,128]{4,1,3,0,2:T(8,128)(2,1)}), bf16[1,128,16,3,128]{4,1,3,0,2:T(8,128)(2,1)S(1)}, u32[]{:S(2)}, u32[]{:S(2)}) async-start(bf16[1,128,16,3,128]{4,1,3,0,2:T(8,128)(2,1)} %bitcast.108), calls=%async_computation.4 | async-start | bytes 3145728 | tf_op jit(solution)/shard_map/all_to_all | solution.py:72
  58.5 51.6 %collective-permute-start = (bf16[1,128,16,3,128]{4,1,3,2,0:T(8,128)(2,1)}, bf16[1,128,16,3,128]{4,1,3,2,0:T(8,128)(2,1)}, u32[]{:S(2)}, u32[]{:S(2)}) collective-permute-start(bf16[1,128,16,3,128]{4,1,3,2,0:T(8,128)(2,1)} %bitcast.7), channel_id=1, source_target_pairs={{0,16},{16,32},{32,48},{48,64},{64,80},{80,96},{96,112},{112,128},... | collective-permute-start | bytes 4718600 | tf_op jit(solution)/shard_map/ppermute | solution.py:12
  110.1 59.6 %all-to-all-start.1 = ((bf16[1,128,16,3,128]{4,1,3,0,2:T(8,128)(2,1)}), bf16[1,128,16,3,128]{4,1,3,0,2:T(8,128)(2,1)}, u32[]{:S(2)}, u32[]{:S(2)}) async-start(bf16[1,128,16,3,128]{4,1,3,0,2:T(8,128)(2,1)} %bitcast.8), calls=%async_computation.1 | async-start | bytes 3145728 | tf_op jit(solution)/shard_map/all_to_all | solution.py:73
  118.3 51.4 %collective-permute-start.1 = (bf16[1,128,16,3,128]{4,1,3,2,0:T(8,128)(2,1)}, bf16[1,128,16,3,128]{4,1,3,2,0:T(8,128)(2,1)}, u32[]{:S(2)}, u32[]{:S(2)}) collective-permute-start(bf16[1,128,16,3,128]{4,1,3,2,0:T(8,128)(2,1)} %bitcast.109), channel_id=1, source_target_pairs={{0,16},{16,32},{32,48},{48,64},{64,80},{80,96},{96,112},{112,128},... | collective-permute-start | bytes 4718600 | tf_op jit(solution)/shard_map/ppermute | solution.py:12
  169.8 44.6 %all-to-all-start.3 = ((bf16[1,128,16,3,128]{4,1,3,0,2:T(8,128)(2,1)}), bf16[1,128,16,3,128]{4,1,3,0,2:T(8,128)(2,1)}, u32[]{:S(2)}, u32[]{:S(2)}) async-start(bf16[1,128,16,3,128]{4,1,3,0,2:T(8,128)(2,1)} %bitcast.17), calls=%async_computation.3 | async-start | bytes 3145728 | tf_op jit(solution)/shard_map/all_to_all | solution.py:74
  178.6 45.2 %copy-start.3 = (s32[1,16]{1,0:T(1,128)S(1)}, s32[1,16]{1,0:T(1,128)}, u32[]{:S(2)}) copy-start(s32[1,16]{1,0:T(1,128)} %param.11) | copy-start | bytes 196
  178.6 45.3 %copy-start.2 = (s32[1,16,32]{2,1,0:T(8,128)S(1)}, s32[1,16,32]{2,1,0:T(8,128)}, u32[]{:S(2)}) copy-start(s32[1,16,32]{2,1,0:T(8,128)} %param.10) | copy-start | bytes 6148
  214.4 42.8 %all-to-all-start = ((bf16[1,128,16,3,128]{4,1,3,0,2:T(8,128)(2,1)}), bf16[1,128,16,3,128]{4,1,3,0,2:T(8,128)(2,1)}, u32[]{:S(2)}, u32[]{:S(2)}) async-start(bf16[1,128,16,3,128]{4,1,3,0,2:T(8,128)(2,1)} %bitcast.107), calls=%async_computation | async-start | bytes 3145728 | tf_op jit(solution)/shard_map/all_to_all | solution.py:70
  280.9 13.7 %copy-start = (bf16[4096,3,128]{2,0,1:T(8,128)(2,1)S(1)}, bf16[4096,3,128]{2,0,1:T(8,128)(2,1)}, u32[]{:S(2)}) copy-start(bf16[4096,3,128]{2,0,1:T(8,128)(2,1)} %get-tuple-element.157) | copy-start | bytes 9437188 | tf_op jit(solution)/shard_map/while
  325.4 13.7 %copy-start = (bf16[4096,3,128]{2,0,1:T(8,128)(2,1)S(1)}, bf16[4096,3,128]{2,0,1:T(8,128)(2,1)}, u32[]{:S(2)}) copy-start(bf16[4096,3,128]{2,0,1:T(8,128)(2,1)} %get-tuple-element.157) | copy-start | bytes 9437188 | tf_op jit(solution)/shard_map/while
  370.0 13.7 %copy-start = (bf16[4096,3,128]{2,0,1:T(8,128)(2,1)S(1)}, bf16[4096,3,128]{2,0,1:T(8,128)(2,1)}, u32[]{:S(2)}) copy-start(bf16[4096,3,128]{2,0,1:T(8,128)(2,1)} %get-tuple-element.157) | copy-start | bytes 9437188 | tf_op jit(solution)/shard_map/while
  414.5 13.7 %copy-start = (bf16[4096,3,128]{2,0,1:T(8,128)(2,1)S(1)}, bf16[4096,3,128]{2,0,1:T(8,128)(2,1)}, u32[]{:S(2)}) copy-start(bf16[4096,3,128]{2,0,1:T(8,128)(2,1)} %get-tuple-element.157) | copy-start | bytes 9437188 | tf_op jit(solution)/shard_map/while
  459.1 13.7 %copy-start = (bf16[4096,3,128]{2,0,1:T(8,128)(2,1)S(1)}, bf16[4096,3,128]{2,0,1:T(8,128)(2,1)}, u32[]{:S(2)}) copy-start(bf16[4096,3,128]{2,0,1:T(8,128)(2,1)} %get-tuple-element.157) | copy-start | bytes 9437188 | tf_op jit(solution)/shard_map/while
  503.6 13.7 %copy-start = (bf16[4096,3,128]{2,0,1:T(8,128)(2,1)S(1)}, bf16[4096,3,128]{2,0,1:T(8,128)(2,1)}, u32[]{:S(2)}) copy-start(bf16[4096,3,128]{2,0,1:T(8,128)(2,1)} %get-tuple-element.157) | copy-start | bytes 9437188 | tf_op jit(solution)/shard_map/while
  548.2 13.7 %copy-start = (bf16[4096,3,128]{2,0,1:T(8,128)(2,1)S(1)}, bf16[4096,3,128]{2,0,1:T(8,128)(2,1)}, u32[]{:S(2)}) copy-start(bf16[4096,3,128]{2,0,1:T(8,128)(2,1)} %get-tuple-element.157) | copy-start | bytes 9437188 | tf_op jit(solution)/shard_map/while
  592.7 13.7 %copy-start = (bf16[4096,3,128]{2,0,1:T(8,128)(2,1)S(1)}, bf16[4096,3,128]{2,0,1:T(8,128)(2,1)}, u32[]{:S(2)}) copy-start(bf16[4096,3,128]{2,0,1:T(8,128)(2,1)} %get-tuple-element.157) | copy-start | bytes 9437188 | tf_op jit(solution)/shard_map/while
where the time goes:
time: 675 us; the launch traced here: 663 us
  waiting for transfers between devices  184 us (27%)
  local copies, waits for them, and re-layouts  147 us (22%)
  matrix products  116 us (17%)
  other arithmetic  115 us (17%)
  starting transfers between devices  56.3 us (8%)
  blocking collectives  43.9 us (7%)
    gather x16, local copies, waits for them, and re-layouts, one_block(): visible = seen_block[:, key_tile][:, None, None, :]  130 us
    sub x8, other arithmetic, one_block(): weights = jnp.where(visible, jnp.exp(masked - largest), 0.0)  109 us
    ppermute x2, waiting for transfers between devices, shifted(): lax.ppermute(value, axis, [(source, source + steps) for source in range(l...  93.8 us
    dot_general x8, matrix products, one_block(): jnp.einsum('gqhd,khd->ghqk', query_block, pool_keys, preferred_element_ty...  58.1 us
    dot_general x8, matrix products, one_block(): jnp.einsum('ghqk,khd->gqhd', weights_bf, pool_values, preferred_element_t...  57.8 us
    all_to_all x1, blocking collectives, per_device(): lax.all_to_all(gathered, 'seq', split_axis=1, concat_axis=2, tiled=True)  43.9 us
    all_to_all x1, waiting for transfers between devices, per_device(): lax.all_to_all(keys_g, 'seq', split_axis=2, concat_axis=1, tiled=True)  33.2 us
    all_to_all x1, waiting for transfers between devices, per_device(): lax.all_to_all(earlier_values, 'seq', split_axis=2, concat_axis=1, tiled=...  32.8 us
  transfers between devices with their start and end apart: 7, of which 5 were waited for; matrix products, arithmetic and copies ran while one was open for 2% of the time, Pallas kernels for 0%

commit v1 on v0

v1 whole, which is shorter than its diff:
```python
import functools
import math

import jax
import jax.numpy as jnp
from jax import lax
from jax.experimental import pallas as pl
from jax.experimental.pallas import tpu as pltpu
from jax.sharding import PartitionSpec as P

MESH = pl.DeviceIdType.MESH
TILE = 128
TILES = 16
TOKENS = TILE * TILES
SPANS = 16
SEQ = 16
HEADS = 48
PER = HEADS // SEQ
WIDTH = 128
QB = 512
KB = 1024
SCALE = math.log2(math.e) / math.sqrt(WIDTH)
HIDDEN = -1e30
CONTRACT_LAST = (((1,), (1,)), ((), ()))
CONTRACT_FIRST = (((0,), (0,)), ((), ()))
CONTRACT_PLAIN = (((1,), (0,)), ((), ()))


def worker_of(span):
    return (span % 8) // 2 * 4 + span // 8 * 2 + span % 2


def span_of(index):
    return (index // 2) % 2 * 8 + index // 4 * 2 + index % 2


def matmul(left, right, dims):
    return lax.dot_general(left, right, dims, preferred_element_type=jnp.float32)


def kernel(
    q_in, k_in, v_in, vis_in, o_out,
    qb, kb, vb, ob, vis, bias, scores,
    in_send, in_recv, vis_send, vis_recv, fwd_send, fwd_recv, o_send, o_recv,
):
    me_span = lax.axis_index("span")
    me_seq = lax.axis_index("seq")
    span = span_of(me_span)
    target = worker_of(me_span)
    after = worker_of(lax.rem(span + 1, SPANS))
    home_works = target == me_span

    ins = (q_in, k_in, v_in)

    def landing(which, head, tile):
        rows = pl.ds(pl.multiple_of(tile * TILE, TILE), TILE)
        own = pl.ds(pl.multiple_of(TOKENS + tile * TILE, TILE), TILE)
        if which == 0:
            return qb.at[head, rows, :]
        if which == 1:
            return kb.at[head, own, :]
        return vb.at[head, :, own]

    def landed(which, head):
        if which == 0:
            return qb.at[head]
        if which == 1:
            return kb.at[head, TOKENS:, :]
        return vb.at[head, :, TOKENS:]

    def peer(step):
        return lax.rem(me_seq + step, SEQ)

    def send_block(which, head, to):
        return pltpu.make_async_remote_copy(
            src_ref=ins[which].at[to * PER + head],
            dst_ref=landing(which, head, me_seq),
            send_sem=in_send.at[which, head],
            recv_sem=in_recv.at[which, head],
            device_id=(target, to),
            device_id_type=MESH,
        )

    def send_vis(to):
        return pltpu.make_async_remote_copy(
            src_ref=vis_in, dst_ref=vis, send_sem=vis_send, recv_sem=vis_recv,
            device_id=(target, to), device_id_type=MESH,
        )

    def send_out(head, tile, to):
        return pltpu.make_async_remote_copy(
            src_ref=ob.at[head, pl.ds(pl.multiple_of(tile * TILE, TILE), TILE), :],
            dst_ref=o_out.at[me_seq * PER + head],
            send_sem=o_send, recv_sem=o_recv,
            device_id=(span, to), device_id_type=MESH,
        )

    def forward(which, head, part):
        rows = pl.ds(part * 512, 512)
        own = pl.ds(TOKENS + part * 512, 512)
        if which == 1:
            src, dst = kb.at[head, own, :], kb.at[head, rows, :]
        else:
            src, dst = vb.at[head, :, own], vb.at[head, :, rows]
        return pltpu.make_async_remote_copy(
            src_ref=src, dst_ref=dst,
            send_sem=fwd_send.at[which - 1, head], recv_sem=fwd_recv.at[which - 1, head],
            device_id=(after, me_seq), device_id_type=MESH,
        )

    @pl.when(span == 0)
    def _():
        kb[:, :TOKENS, :] = jnp.zeros((PER, TOKENS, WIDTH), jnp.bfloat16)
        vb[:, :, :TOKENS] = jnp.zeros((PER, WIDTH, TOKENS), jnp.bfloat16)

    @pl.when(home_works)
    def _():
        pltpu.make_async_copy(vis_in, vis, vis_recv).start()

    @pl.when(jnp.logical_not(home_works))
    def _():
        send_vis(me_seq).start()

    for head in range(PER):
        for which in (1, 2, 0):
            @pl.loop(1, SEQ)
            def _(step):
                send_block(which, head, peer(step)).start()

            @pl.when(home_works)
            def _():
                pltpu.make_async_copy(
                    ins[which].at[me_seq * PER + head],
                    landing(which, head, me_seq),
                    in_recv.at[which, head],
                ).start()

            @pl.when(jnp.logical_not(home_works))
            def _():
                send_block(which, head, me_seq).start()

    pltpu.make_async_copy(vis, vis, vis_recv).wait()
    tile_of = lax.broadcasted_iota(jnp.int32, (TILE, TOKENS), 1) // TILE
    pick = (tile_of == lax.broadcasted_iota(jnp.int32, (TILE, TOKENS), 0)).astype(jnp.bfloat16)
    seen = matmul(vis[...].astype(jnp.bfloat16), pick, CONTRACT_PLAIN)
    bias[...] = (1.0 - seen) * HIDDEN

    for head in range(PER):
        for which in (1, 2):
            pltpu.make_async_copy(
                landed(which, head), landed(which, head), in_recv.at[which, head]
            ).wait()

            @pl.when(span != SPANS - 1)
            def _():
                for part in range(4):
                    forward(which, head, part).start()

        pltpu.make_async_copy(landed(0, head), landed(0, head), in_recv.at[0, head]).wait()

        @pl.when(span != 0)
        def _():
            for which, prev in ((1, kb.at[head, :TOKENS, :]), (2, vb.at[head, :, :TOKENS])):
                pltpu.make_async_copy(prev, prev, fwd_recv.at[which - 1, head]).wait()

        @pl.loop(0, TOKENS // QB)
        def _(block):
            start = pl.multiple_of(block * QB, QB)
            columns = pl.ds(start, QB)
            query = qb[head, columns, :]
            chunks = TOKENS // KB + (block * QB + QB + KB - 1) // KB

            def score(chunk, largest):
                first = pl.multiple_of(chunk * KB, KB)
                part = matmul(kb[head, pl.ds(first, KB), :], query, CONTRACT_LAST)
                scores[pl.ds(first, KB), :] = part
                for tile in range(KB // TILE):
                    rows = part[tile * TILE:(tile + 1) * TILE].reshape(TILE // 8, 8, QB)
                    hidden = bias[pl.ds(chunk * (KB // TILE) + tile, 1), columns]
                    largest = jnp.maximum(largest, jnp.max(rows, axis=0) + hidden)
                return largest

            largest = lax.fori_loop(0, chunks, score, jnp.full((8, QB), -3e38, jnp.float32))
            top = jnp.max(largest, axis=0, keepdims=True) * SCALE

            def weigh(chunk, carry):
                total, summed = carry
                first = pl.multiple_of(chunk * KB, KB)
                parts = []
                for tile in range(KB // TILE):
                    hidden = bias[pl.ds(chunk * (KB // TILE) + tile, 1), columns]
                    rows = scores[pl.ds(first + tile * TILE, TILE), :]
                    weight = jnp.exp2(rows * SCALE - (top - hidden))
                    summed = summed + jnp.sum(weight.reshape(TILE // 8, 8, QB), axis=0)
                    parts.append(weight.astype(jnp.bfloat16))
                weights = jnp.concatenate(parts, 0)
                total = total + matmul(vb[head, :, pl.ds(first, KB)], weights, CONTRACT_PLAIN)
                return total, summed

            total, summed = lax.fori_loop(
                0, chunks, weigh,
                (jnp.zeros((WIDTH, QB), jnp.float32), jnp.zeros((8, QB), jnp.float32)),
            )
            result = total / jnp.sum(summed, axis=0, keepdims=True)
            ob[head, columns, :] = jnp.transpose(result).astype(jnp.bfloat16)

            for part in range(QB // TILE):
                tile = block * (QB // TILE) + part
                here = jnp.logical_and(span == me_span, tile == me_seq)

                @pl.when(here)
                def _():
                    pltpu.make_async_copy(
                        ob.at[head, pl.ds(pl.multiple_of(tile * TILE, TILE), TILE), :],
                        o_out.at[me_seq * PER + head],
                        o_recv,
                    ).start()

                @pl.when(jnp.logical_not(here))
                def _():
                    send_out(head, tile, tile).start()

    pltpu.make_async_copy(o_out, o_out, o_recv).wait()

    for head in range(PER):
        for which in (0, 1, 2):
            sent = ins[which].at[: SEQ - 1]
            pltpu.make_async_copy(sent, sent, in_send.at[which, head]).wait()

            @pl.when(jnp.logical_not(home_works))
            def _():
                send_block(which, head, me_seq).wait_send()

        @pl.when(span != SPANS - 1)
        def _():
            for which, own in ((1, kb.at[head, TOKENS:, :]), (2, vb.at[head, :, TOKENS:])):
                pltpu.make_async_copy(own, own, fwd_send.at[which - 1, head]).wait()

    @pl.when(jnp.logical_not(home_works))
    def _():
        send_vis(me_seq).wait_send()

    sent = o_out.at[: HEADS - PER]
    pltpu.make_async_copy(sent, sent, o_send).wait()

    @pl.when(span != me_span)
    def _():
        last = o_out.at[:PER]
        pltpu.make_async_copy(last, last, o_send).wait()


def exchange_and_attend(query, keys, values, visible):
    anywhere = pl.BlockSpec(memory_space=pl.ANY)
    return pl.pallas_call(
        kernel,
        out_shape=jax.ShapeDtypeStruct((HEADS, TILE, WIDTH), jnp.bfloat16),
        in_specs=[anywhere] * 4,
        out_specs=anywhere,
        scratch_shapes=[
            pltpu.VMEM((PER, TOKENS, WIDTH), jnp.bfloat16),
            pltpu.VMEM((PER, 2 * TOKENS, WIDTH), jnp.bfloat16),
            pltpu.VMEM((PER, WIDTH, 2 * TOKENS), jnp.bfloat16),
            pltpu.VMEM((PER, TOKENS, WIDTH), jnp.bfloat16),
            pltpu.VMEM((2 * TILES, TILE), jnp.float32),
            pltpu.VMEM((2 * TILES, TOKENS), jnp.float32),
            pltpu.VMEM((2 * TOKENS, QB), jnp.float32),
            pltpu.SemaphoreType.DMA((3, PER)),
            pltpu.SemaphoreType.DMA((3, PER)),
            pltpu.SemaphoreType.DMA,
            pltpu.SemaphoreType.DMA,
            pltpu.SemaphoreType.DMA((2, PER)),
            pltpu.SemaphoreType.DMA((2, PER)),
            pltpu.SemaphoreType.DMA,
            pltpu.SemaphoreType.DMA,
        ],
        compiler_params=pltpu.CompilerParams(
            vmem_limit_bytes=56 << 20, has_side_effects=True
        ),
        name="exchange_and_attend",
    )(query, keys, values, visible)


def visible_tiles(tile_lists, tile_counts):
    slots = jnp.arange(2 * TILES, dtype=jnp.int32)
    used = slots[None, :] < tile_counts[:, None]
    named = (tile_lists[:, :, None] == slots[None, None, :]) & used[:, :, None]
    return jnp.any(named, axis=1).T.astype(jnp.float32)


def per_device(query, keys, values, block_list, block_count):
    visible = jnp.pad(
        visible_tiles(block_list[0], block_count[0]), ((0, 0), (0, TILE - TILES))
    )
    result = exchange_and_attend(
        jnp.transpose(query[0], (1, 0, 2)),
        jnp.transpose(keys[0], (1, 0, 2)),
        jnp.transpose(values[0], (1, 2, 0)),
        visible,
    )
    return jnp.transpose(result, (1, 0, 2))[None]


def solution(mesh):
    in_specs = (
        P("span", "seq", None, None),
        P("span", "seq", None, None),
        P("span", "seq", None, None),
        P("span", None, None),
        P("span", None),
    )
    out_specs = P("span", "seq", None, None)
    return jax.shard_map(
        per_device, mesh=mesh, in_specs=in_specs, out_specs=out_specs, check_vma=False
    )
```

time: 675 us -> 256 us (0.38)
  the two profiles are of different devices: /device:TPU:11 before, /device:TPU:208 now
where the time goes in v1:
time: 256 us
  Pallas kernels  244 us (95%)
  local copies, waits for them, and re-layouts  9.3 us (4%)
    pallas_call x1, Pallas kernels, exchange_and_attend(): pl.pallas_call(kernel, out_shape=jax.ShapeDtypeStruct((HEADS, TILE, WIDTH...  244 us

profile of v1, /device:TPU:208, one launch (start us, length us, event | category | flops | bytes accessed | tf_op | source)
XLA Modules:
  0.0 255.8 jit_solution(6805302968763488915)
XLA Ops:
  0.0 0.7 iota_compare_fusion.1
  0.7 0.9 fusion.1
  1.6 0.1 copy.13
  1.7 0.6 pad_convert_fusion.vis_in
  2.4 0.0 copy-start
  2.4 0.0 copy-start.1
  2.4 3.0 %copy.12 = bf16[1,128,48,128]{1,3,2,0:T(8,128)(2,1)} copy(bf16[1,128,48,128]{3,2,1,0:T(8,128)(2,1)} %param.7) | data formatting | bytes 3145728 | tf_op args[2]
  5.3 0.0 copy-done
  5.3 0.0 copy-done.1
  5.4 2.6 %copy_bitcast_fusion = (bf16[48,128,128]{2,1,0:T(8,128)(2,1)}, bf16[48,128,128]{2,1,0:T(8,128)(2,1)}) fusion(bf16[1,128,48,128]{3,2,1,0:T(8,128)(2,1)S(1)} %copy-done, bf16[1,128,48,128]{3,2,1,0:T(8,128)(2,1)S(1)} %copy-done.1), kind=kLoop, calls=%fused_computation | loop fusion | bytes 6291456 | tf_op jit(solution)/shard_map/transpose | solution.py:296
  8.0 244.2 %exchange_and_attend.1 = bf16[48,128,128]{2,1,0:T(8,128)(2,1)} custom-call(bf16[48,128,128]{2,1,0:T(8,128)(2,1)} %get-tuple-element.6.q_in, bf16[48,128,128]{2,1,0:T(8,128)(2,1)} %get-tuple-element.5.k_in, bf16[48,128,128]{2,1,0:T(8,128)(2,1)} %bitcast.17, f32[32,128]{1,0:T(8,128)} %pad_convert_fusion.vis_in), custom_call_target="tpu_custom_call" | custom-call | tf_op jit(solution)/shard_map/exchange_and_attend/pallas_call | solution.py:254
  252.2 3.6 %copy.14 = bf16[1,128,48,128]{3,2,1,0:T(8,128)(2,1)} copy(bf16[1,128,48,128]{3,1,2,0:T(8,128)(2,1)} %bitcast.18) | data formatting | bytes 3145728 | tf_op jit(solution)/shard_map/broadcast_in_dim | solution.py:300
Async XLA Ops:
  2.4 3.0 %copy-start = (bf16[1,128,48,128]{3,2,1,0:T(8,128)(2,1)S(1)}, bf16[1,128,48,128]{3,2,1,0:T(8,128)(2,1)}, u32[]{:S(2)}) copy-start(bf16[1,128,48,128]{3,2,1,0:T(8,128)(2,1)} %param.6) | copy-start | bytes 4718596
  2.4 3.0 %copy-start.1 = (bf16[1,128,48,128]{3,2,1,0:T(8,128)(2,1)S(1)}, bf16[1,128,48,128]{3,2,1,0:T(8,128)(2,1)}, u32[]{:S(2)}) copy-start(bf16[1,128,48,128]{3,2,1,0:T(8,128)(2,1)} %param.5) | copy-start | bytes 4718596

commit v2 on v1

v2 whole, which is shorter than its diff:
```python
import functools
import math

import jax
import jax.numpy as jnp
from jax import lax
from jax.experimental import pallas as pl
from jax.experimental.pallas import tpu as pltpu
from jax.sharding import PartitionSpec as P

MESH = pl.DeviceIdType.MESH
TILE = 128
TILES = 16
TOKENS = TILE * TILES
SPANS = 16
SEQ = 16
HEADS = 48
PER = HEADS // SEQ
WIDTH = 128
QB = 512
KB = 1024
SCALE = math.log2(math.e) / math.sqrt(WIDTH)
HIDDEN = -1e30
CONTRACT_LAST = (((1,), (1,)), ((), ()))
CONTRACT_FIRST = (((0,), (0,)), ((), ()))
CONTRACT_PLAIN = (((1,), (0,)), ((), ()))


def matmul(left, right, dims):
    return lax.dot_general(left, right, dims, preferred_element_type=jnp.float32)


def kernel(
    q_in, k_in, v_in, vis_in, o_out,
    qb, kb, vb, ob, vis, bias, scores,
    in_send, in_recv, vis_send, vis_recv, fwd_send, fwd_recv, o_send, o_recv,
):
    me_span = lax.axis_index("span")
    me_seq = lax.axis_index("seq")
    row = me_span // 4
    local = lax.rem(me_span, 4)
    core = lax.rem(me_span, 2)
    plane = lax.rem(me_span // 2, 2)
    x = lax.rem(me_seq, 4)
    side = lax.rem(x, 2)
    z = me_seq // 4 * 2 + plane
    me_group = x // 2 * 8 + z
    item_spans = (2 * core, 2 * core + 1, 2 * side + core)
    item_heads = (3 * me_group + side, 3 * me_group + side, 3 * me_group + 2)

    ins = (q_in, k_in, v_in)
    base = (0, 1, 3)

    def place(which, slot, tile):
        at = pl.ds(pl.multiple_of(slot * TOKENS + tile * TILE, TILE), TILE)
        if which == 0:
            return qb.at[at, :]
        if which == 1:
            return kb.at[at, :]
        return vb.at[:, at]

    def slot_ref(which, slot):
        at = pl.ds(slot * TOKENS, TOKENS)
        if which == 0:
            return qb.at[at, :]
        if which == 1:
            return kb.at[at, :]
        return vb.at[:, at]

    def item_slot(which, item):
        return item if which == 0 else base[item] + 1

    def chip(group, x_side, its_core):
        its_z = lax.rem(group, 8)
        return (
            row * 4 + lax.rem(its_z, 2) * 2 + its_core,
            its_z // 2 * 4 + group // 8 * 2 + x_side,
        )

    def major_block(which, step, x_side):
        group = lax.rem(me_group + step, 16)
        item = lax.rem(local, 2)
        slot = item if which == 0 else 1 + item
        return pltpu.make_async_remote_copy(
            src_ref=ins[which].at[3 * group + x_side],
            dst_ref=place(which, slot, me_seq),
            send_sem=in_send.at[which, 0], recv_sem=in_recv.at[which, item],
            device_id=chip(group, x_side, local // 2), device_id_type=MESH,
        )

    def shared_block(which, step):
        group = lax.rem(me_group + step, 16)
        return pltpu.make_async_remote_copy(
            src_ref=ins[which].at[3 * group + 2],
            dst_ref=place(which, item_slot(which, 2), me_seq),
            send_sem=in_send.at[which, 1], recv_sem=in_recv.at[which, 2],
            device_id=chip(group, local // 2, lax.rem(local, 2)), device_id_type=MESH,
        )

    major_home = local // 2 == core
    shared_home = local // 2 == side

    def start_major(which):
        item = lax.rem(local, 2)
        slot = item if which == 0 else 1 + item

        @pl.when(major_home)
        def _():
            pltpu.make_async_copy(
                ins[which].at[3 * me_group + side],
                place(which, slot, me_seq),
                in_recv.at[which, item],
            ).start()

        @pl.when(jnp.logical_not(major_home))
        def _():
            major_block(which, 0, side).start()

        major_block(which, 0, 1 - side).start()

        @pl.loop(1, 16)
        def _(step):
            major_block(which, step, side).start()
            major_block(which, step, 1 - side).start()

    def start_shared(which):
        @pl.when(shared_home)
        def _():
            pltpu.make_async_copy(
                ins[which].at[3 * me_group + 2],
                place(which, item_slot(which, 2), me_seq),
                in_recv.at[which, 2],
            ).start()

        @pl.when(jnp.logical_not(shared_home))
        def _():
            shared_block(which, 0).start()

        @pl.loop(1, 16)
        def _(step):
            shared_block(which, step).start()

    def wait_item(which, item):
        ref = slot_ref(which, item_slot(which, item))
        pltpu.make_async_copy(ref, ref, in_recv.at[which, item]).wait()

    next_row = lax.rem(row + 1, 4)
    fwd_span = jnp.where(core == 0, me_span + 1, next_row * 4 + plane * 2)
    shared_row = jnp.where(side == 0, row, next_row)
    fwd_shared_span = jnp.where(core == 0, me_span + 1, shared_row * 4 + plane * 2)
    fwd_shared_seq = jnp.where(core == 0, me_seq, jnp.where(side == 0, me_seq + 1, me_seq - 1))
    last_row = row == 3
    fwd_major_sends = jnp.logical_not(jnp.logical_and(core == 1, last_row))
    fwd_shared_sends = jnp.logical_not(
        jnp.logical_and(jnp.logical_and(core == 1, side == 1), last_row)
    )
    first_row = jnp.logical_and(core == 0, row == 0)
    major_first = first_row
    shared_first = jnp.logical_and(first_row, side == 0)

    def forward(which, shared):
        return pltpu.make_async_remote_copy(
            src_ref=slot_ref(which, 4 if shared else 2),
            dst_ref=slot_ref(which, 3 if shared else 0),
            send_sem=fwd_send.at[which - 1, shared], recv_sem=fwd_recv.at[which - 1, shared],
            device_id=(fwd_shared_span, fwd_shared_seq) if shared else (fwd_span, me_seq),
            device_id_type=MESH,
        )

    def vis_block(offset):
        return pltpu.make_async_remote_copy(
            src_ref=vis_in, dst_ref=vis.at[local],
            send_sem=vis_send, recv_sem=vis_recv,
            device_id=(row * 4 + lax.rem(local + offset, 4), me_seq), device_id_type=MESH,
        )

    for offset in range(1, 4):
        vis_block(offset).start()
    pltpu.make_async_copy(vis_in, vis.at[local], vis_recv).start()
    for which in (1, 2, 0):
        start_shared(which)

    @pl.when(major_first)
    def _():
        kb[:TOKENS, :] = jnp.zeros((TOKENS, WIDTH), jnp.bfloat16)
        vb[:, :TOKENS] = jnp.zeros((WIDTH, TOKENS), jnp.bfloat16)

    @pl.when(shared_first)
    def _():
        kb[3 * TOKENS:4 * TOKENS, :] = jnp.zeros((TOKENS, WIDTH), jnp.bfloat16)
        vb[:, 3 * TOKENS:4 * TOKENS] = jnp.zeros((WIDTH, TOKENS), jnp.bfloat16)

    pltpu.make_async_copy(vis, vis, vis_recv).wait()
    tile_of = lax.broadcasted_iota(jnp.int32, (TILE, TOKENS), 1) // TILE
    pick = (tile_of == lax.broadcasted_iota(jnp.int32, (TILE, TOKENS), 0)).astype(jnp.bfloat16)
    for item in range(PER):
        seen = matmul(vis[item_spans[item]].astype(jnp.bfloat16), pick, CONTRACT_PLAIN)
        bias[item] = (1.0 - seen) * HIDDEN

    def attend(item):
        origin = base[item] * TOKENS

        @pl.loop(0, TOKENS // QB)
        def _(block):
            start = pl.multiple_of(block * QB, QB)
            columns = pl.ds(start, QB)
            query = qb[pl.ds(pl.multiple_of(item * TOKENS + start, QB), QB), :]
            chunks = TOKENS // KB + (block * QB + QB + KB - 1) // KB

            def score(chunk, largest):
                first = pl.multiple_of(chunk * KB, KB)
                part = matmul(kb[pl.ds(origin + first, KB), :], query, CONTRACT_LAST)
                scores[pl.ds(first, KB), :] = part
                for tile in range(KB // TILE):
                    rows = part[tile * TILE:(tile + 1) * TILE].reshape(TILE // 8, 8, QB)
                    hidden = bias[item, pl.ds(chunk * (KB // TILE) + tile, 1), columns]
                    largest = jnp.maximum(largest, jnp.max(rows, axis=0) + hidden)
                return largest

            largest = lax.fori_loop(0, chunks, score, jnp.full((8, QB), -3e38, jnp.float32))
            top = jnp.max(largest, axis=0, keepdims=True) * SCALE

            def weigh(chunk, carry):
                total, summed = carry
                first = pl.multiple_of(chunk * KB, KB)
                parts = []
                for tile in range(KB // TILE):
                    hidden = bias[item, pl.ds(chunk * (KB // TILE) + tile, 1), columns]
                    rows = scores[pl.ds(first + tile * TILE, TILE), :]
                    weight = jnp.exp2(rows * SCALE - (top - hidden))
                    summed = summed + jnp.sum(weight.reshape(TILE // 8, 8, QB), axis=0)
                    parts.append(weight.astype(jnp.bfloat16))
                weights = jnp.concatenate(parts, 0)
                total = total + matmul(vb[:, pl.ds(origin + first, KB)], weights, CONTRACT_PLAIN)
                return total, summed

            total, summed = lax.fori_loop(
                0, chunks, weigh,
                (jnp.zeros((WIDTH, QB), jnp.float32), jnp.zeros((8, QB), jnp.float32)),
            )
            result = total / jnp.sum(summed, axis=0, keepdims=True)
            ob[item, columns, :] = jnp.transpose(result).astype(jnp.bfloat16)

            for part in range(QB // TILE):
                tile = block * (QB // TILE) + part
                source = ob.at[item, pl.ds(pl.multiple_of(tile * TILE, TILE), TILE), :]
                here = jnp.logical_and(item_spans[item] == local, tile == me_seq)

                @pl.when(here)
                def _():
                    pltpu.make_async_copy(source, o_out.at[item_heads[item]], o_recv).start()

                @pl.when(jnp.logical_not(here))
                def _():
                    pltpu.make_async_remote_copy(
                        src_ref=source, dst_ref=o_out.at[item_heads[item]],
                        send_sem=o_send.at[item], recv_sem=o_recv,
                        device_id=(row * 4 + item_spans[item], tile), device_id_type=MESH,
                    ).start()

    for which in (1, 2):
        wait_item(which, 2)

        @pl.when(fwd_shared_sends)
        def _():
            forward(which, 1).start()

    start_major(1)
    start_major(2)
    wait_item(0, 2)

    @pl.when(jnp.logical_not(shared_first))
    def _():
        for which in (1, 2):
            ref = slot_ref(which, 3)
            pltpu.make_async_copy(ref, ref, fwd_recv.at[which - 1, 1]).wait()

    attend(2)

    for which in (1, 2):
        wait_item(which, 1)

        @pl.when(fwd_major_sends)
        def _():
            forward(which, 0).start()

    start_major(0)
    for which in (1, 2, 0):
        wait_item(which, 0)

    @pl.when(jnp.logical_not(major_first))
    def _():
        for which in (1, 2):
            ref = slot_ref(which, 0)
            pltpu.make_async_copy(ref, ref, fwd_recv.at[which - 1, 0]).wait()

    attend(0)
    wait_item(0, 1)
    attend(1)

    pltpu.make_async_copy(o_out, o_out, o_recv).wait()

    for offset in range(1, 4):
        vis_block(offset).wait_send()
    for which in (0, 1, 2):
        sent = ins[which].at[:31]
        pltpu.make_async_copy(sent, sent, in_send.at[which, 0]).wait()
        sent = ins[which].at[:15]
        pltpu.make_async_copy(sent, sent, in_send.at[which, 1]).wait()

        @pl.when(jnp.logical_not(major_home))
        def _():
            major_block(which, 0, side).wait_send()

        @pl.when(jnp.logical_not(shared_home))
        def _():
            shared_block(which, 0).wait_send()

    @pl.when(fwd_major_sends)
    def _():
        for which in (1, 2):
            forward(which, 0).wait_send()

    @pl.when(fwd_shared_sends)
    def _():
        for which in (1, 2):
            forward(which, 1).wait_send()

    for item in range(PER):
        sent = o_out.at[:15]
        pltpu.make_async_copy(sent, sent, o_send.at[item]).wait()

        @pl.when(item_spans[item] != local)
        def _():
            last = o_out.at[0]
            pltpu.make_async_copy(last, last, o_send.at[item]).wait()


def exchange_and_attend(query, keys, values, visible):
    anywhere = pl.BlockSpec(memory_space=pl.ANY)
    return pl.pallas_call(
        kernel,
        out_shape=jax.ShapeDtypeStruct((HEADS, TILE, WIDTH), jnp.bfloat16),
        in_specs=[anywhere] * 4,
        out_specs=anywhere,
        scratch_shapes=[
            pltpu.VMEM((PER * TOKENS, WIDTH), jnp.bfloat16),
            pltpu.VMEM((5 * TOKENS, WIDTH), jnp.bfloat16),
            pltpu.VMEM((WIDTH, 5 * TOKENS), jnp.bfloat16),
            pltpu.VMEM((PER, TOKENS, WIDTH), jnp.bfloat16),
            pltpu.VMEM((4, 2 * TILES, TILE), jnp.float32),
            pltpu.VMEM((PER, 2 * TILES, TOKENS), jnp.float32),
            pltpu.VMEM((2 * TOKENS, QB), jnp.float32),
            pltpu.SemaphoreType.DMA((3, 2)),
            pltpu.SemaphoreType.DMA((3, PER)),
            pltpu.SemaphoreType.DMA,
            pltpu.SemaphoreType.DMA,
            pltpu.SemaphoreType.DMA((2, 2)),
            pltpu.SemaphoreType.DMA((2, 2)),
            pltpu.SemaphoreType.DMA((PER,)),
            pltpu.SemaphoreType.DMA,
        ],
        compiler_params=pltpu.CompilerParams(
            vmem_limit_bytes=56 << 20, has_side_effects=True
        ),
        name="exchange_and_attend",
    )(query, keys, values, visible)


def visible_tiles(tile_lists, tile_counts):
    slots = jnp.arange(2 * TILES, dtype=jnp.int32)
    used = slots[None, :] < tile_counts[:, None]
    named = (tile_lists[:, :, None] == slots[None, None, :]) & used[:, :, None]
    return jnp.any(named, axis=1).T.astype(jnp.float32)


def per_device(query, keys, values, block_list, block_count):
    visible = jnp.pad(
        visible_tiles(block_list[0], block_count[0]), ((0, 0), (0, TILE - TILES))
    )
    result = exchange_and_attend(
        jnp.transpose(query[0], (1, 0, 2)),
        jnp.transpose(keys[0], (1, 0, 2)),
        jnp.transpose(values[0], (1, 2, 0)),
        visible,
    )
    return jnp.transpose(result, (1, 0, 2))[None]


def solution(mesh):
    in_specs = (
        P("span", "seq", None, None),
        P("span", "seq", None, None),
        P("span", "seq", None, None),
        P("span", None, None),
        P("span", None),
    )
    out_specs = P("span", "seq", None, None)
    return jax.shard_map(
        per_device, mesh=mesh, in_specs=in_specs, out_specs=out_specs, check_vma=False
    )
```

time: 256 us -> 185 us (0.72)
  the two profiles are of different devices: /device:TPU:208 before, /device:TPU:11 now
where the time goes in v2:
time: 185 us; the launch traced here: 184 us
  Pallas kernels  172 us (93%)
  local copies, waits for them, and re-layouts  9.3 us (5%)
  other arithmetic  2.25 us (1%)
    pallas_call x1, Pallas kernels, exchange_and_attend(): pl.pallas_call(kernel, out_shape=jax.ShapeDtypeStruct((HEADS, TILE, WIDTH...  172 us

profile of v2, /device:TPU:11, one launch (start us, length us, event | category | flops | bytes accessed | tf_op | source)
XLA Modules:
  0.0 183.9 jit_solution(4230441139284744263)
XLA Ops:
  0.0 0.7 iota_compare_fusion.1
  0.7 0.9 fusion.1
  1.6 0.1 copy.13
  1.7 0.6 pad_convert_fusion.vis_in
  2.4 0.0 copy-start
  2.4 0.0 copy-start.1
  2.4 3.0 %copy.12 = bf16[1,128,48,128]{1,3,2,0:T(8,128)(2,1)} copy(bf16[1,128,48,128]{3,2,1,0:T(8,128)(2,1)} %param.7) | data formatting | bytes 3145728 | tf_op args[2]
  5.3 0.0 copy-done
  5.3 0.0 copy-done.1
  5.4 2.6 %copy_bitcast_fusion = (bf16[48,128,128]{2,1,0:T(8,128)(2,1)}, bf16[48,128,128]{2,1,0:T(8,128)(2,1)}) fusion(bf16[1,128,48,128]{3,2,1,0:T(8,128)(2,1)S(1)} %copy-done, bf16[1,128,48,128]{3,2,1,0:T(8,128)(2,1)S(1)} %copy-done.1), kind=kLoop, calls=%fused_computation | loop fusion | bytes 6291456 | tf_op jit(solution)/shard_map/transpose | solution.py:383
  8.0 172.3 %exchange_and_attend.1 = bf16[48,128,128]{2,1,0:T(8,128)(2,1)} custom-call(bf16[48,128,128]{2,1,0:T(8,128)(2,1)} %get-tuple-element.6.q_in, bf16[48,128,128]{2,1,0:T(8,128)(2,1)} %get-tuple-element.5.k_in, bf16[48,128,128]{2,1,0:T(8,128)(2,1)} %bitcast.17, f32[32,128]{1,0:T(8,128)} %pad_convert_fusion.vis_in), custom_call_target="tpu_custom_call" | custom-call | tf_op jit(solution)/shard_map/exchange_and_attend/pallas_call | solution.py:341
  180.3 3.6 %copy.14 = bf16[1,128,48,128]{3,2,1,0:T(8,128)(2,1)} copy(bf16[1,128,48,128]{3,1,2,0:T(8,128)(2,1)} %bitcast.18) | data formatting | bytes 3145728 | tf_op jit(solution)/shard_map/broadcast_in_dim | solution.py:387
Async XLA Ops:
  2.4 3.0 %copy-start = (bf16[1,128,48,128]{3,2,1,0:T(8,128)(2,1)S(1)}, bf16[1,128,48,128]{3,2,1,0:T(8,128)(2,1)}, u32[]{:S(2)}) copy-start(bf16[1,128,48,128]{3,2,1,0:T(8,128)(2,1)} %param.6) | copy-start | bytes 4718596
  2.4 3.0 %copy-start.1 = (bf16[1,128,48,128]{3,2,1,0:T(8,128)(2,1)S(1)}, bf16[1,128,48,128]{3,2,1,0:T(8,128)(2,1)}, u32[]{:S(2)}) copy-start(bf16[1,128,48,128]{3,2,1,0:T(8,128)(2,1)} %param.5) | copy-start | bytes 4718596

commit v3 on v2

--- a/solution.py
+++ b/solution.py
@@ -31,8 +31,8 @@
 
 
 def kernel(
-    q_in, k_in, v_in, vis_in, o_out,
-    qb, kb, vb, ob, vis, bias, scores,
+    q_raw, k_raw, v_raw, list_in, count_in, o_out,
+    loaded, ins, arrived, vis_in, qb, kb, vb, ob, vis, bias, scores, load,
     in_send, in_recv, vis_send, vis_recv, fwd_send, fwd_recv, o_send, o_recv,
 ):
     me_span = lax.axis_index("span")
@@ -48,7 +48,6 @@
     item_spans = (2 * core, 2 * core + 1, 2 * side + core)
     item_heads = (3 * me_group + side, 3 * me_group + side, 3 * me_group + 2)
 
-    ins = (q_in, k_in, v_in)
     base = (0, 1, 3)
 
     def place(which, slot, tile):
@@ -82,7 +81,7 @@
         item = lax.rem(local, 2)
         slot = item if which == 0 else 1 + item
         return pltpu.make_async_remote_copy(
-            src_ref=ins[which].at[3 * group + x_side],
+            src_ref=ins.at[which, 3 * group + x_side],
             dst_ref=place(which, slot, me_seq),
             send_sem=in_send.at[which, 0], recv_sem=in_recv.at[which, item],
             device_id=chip(group, x_side, local // 2), device_id_type=MESH,
@@ -91,7 +90,7 @@
     def shared_block(which, step):
         group = lax.rem(me_group + step, 16)
         return pltpu.make_async_remote_copy(
-            src_ref=ins[which].at[3 * group + 2],
+            src_ref=ins.at[which, 3 * group + 2],
             dst_ref=place(which, item_slot(which, 2), me_seq),
             send_sem=in_send.at[which, 1], recv_sem=in_recv.at[which, 2],
             device_id=chip(group, local // 2, lax.rem(local, 2)), device_id_type=MESH,
@@ -107,7 +106,7 @@
         @pl.when(major_home)
         def _():
             pltpu.make_async_copy(
-                ins[which].at[3 * me_group + side],
+                ins.at[which, 3 * me_group + side],
                 place(which, slot, me_seq),
                 in_recv.at[which, item],
             ).start()
@@ -127,7 +126,7 @@
         @pl.when(shared_home)
         def _():
             pltpu.make_async_copy(
-                ins[which].at[3 * me_group + 2],
+                ins.at[which, 3 * me_group + 2],
                 place(which, item_slot(which, 2), me_seq),
                 in_recv.at[which, 2],
             ).start()
@@ -174,11 +173,67 @@
             device_id=(row * 4 + lax.rem(local + offset, 4), me_seq), device_id_type=MESH,
         )
 
+    loads = [
+        pltpu.make_async_copy(raw, loaded.at[which], load.at[which])
+        for which, raw in enumerate((q_raw, k_raw, v_raw))
+    ]
+    for which in (1, 2, 0):
+        loads[which].start()
+
+    barrier = pltpu.get_barrier_semaphore()
+
+    @pl.loop(1, 64)
+    def _(step):
+        other = lax.rem(local * 16 + me_seq + step, 64)
+        pl.semaphore_signal(
+            barrier, inc=1, device_id=(row * 4 + other // 16, lax.rem(other, 16)),
+            device_id_type=MESH,
+        )
+
+    row_before = lax.rem(row + 3, 4) * 4 + plane * 2 + 1
+
+    @pl.when(core == 0)
+    def _():
+        pl.semaphore_signal(
+            barrier, inc=1, device_id=(row_before, me_seq), device_id_type=MESH
+        )
+
+    @pl.when(jnp.logical_and(core == 0, side == 0))
+    def _():
+        pl.semaphore_signal(
+            barrier, inc=1, device_id=(row_before, me_seq + 1), device_id_type=MESH
+        )
+
+    column = lax.broadcasted_iota(jnp.int32, (TILES, TILE), 1)
+    diagonal = lax.broadcasted_iota(jnp.int32, (TILES, TILES), 0) == lax.broadcasted_iota(
+        jnp.int32, (TILES, TILES), 1
+    )
+    count = jnp.sum(
+        jnp.where(diagonal, count_in[...].astype(jnp.float32), 0.0), axis=1, keepdims=True
+    )
+    seen = jnp.zeros((TILES, TILE), jnp.float32)
+    for slot in range(2 * TILES):
+        named = jnp.logical_and(list_in[:, slot:slot + 1] == column, count > slot)
+        seen = jnp.where(named, 1.0, seen)
+    vis_in[...] = seen
+
+    for which in (1, 2, 0):
+        loads[which].wait()
+        ins[which] = jnp.transpose(loaded[which], (1, 0, 2))
+        if which == 2:
+            @pl.loop(0, HEADS // 4)
+            def _(four):
+                for part in range(4):
+                    ins[2, 4 * four + part] = jnp.transpose(ins[2, 4 * four + part])
+
+    pl.semaphore_wait(barrier, 63 + core * (1 + side))
+
     for offset in range(1, 4):
         vis_block(offset).start()
     pltpu.make_async_copy(vis_in, vis.at[local], vis_recv).start()
-    for which in (1, 2, 0):
+    for which in (1, 2):
         start_shared(which)
+    start_major(1)
 
     @pl.when(major_first)
     def _():
@@ -191,11 +246,11 @@
         vb[:, 3 * TOKENS:4 * TOKENS] = jnp.zeros((WIDTH, TOKENS), jnp.bfloat16)
 
     pltpu.make_async_copy(vis, vis, vis_recv).wait()
-    tile_of = lax.broadcasted_iota(jnp.int32, (TILE, TOKENS), 1) // TILE
-    pick = (tile_of == lax.broadcasted_iota(jnp.int32, (TILE, TOKENS), 0)).astype(jnp.bfloat16)
+    tile_of = lax.broadcasted_iota(jnp.int32, (TILES, TOKENS), 1) // TILE
+    pick = (tile_of == lax.broadcasted_iota(jnp.int32, (TILES, TOKENS), 0)).astype(jnp.bfloat16)
     for item in range(PER):
-        seen = matmul(vis[item_spans[item]].astype(jnp.bfloat16), pick, CONTRACT_PLAIN)
-        bias[item] = (1.0 - seen) * HIDDEN
+        seen = matmul(vis[item_spans[item]].astype(jnp.bfloat16), pick, CONTRACT_FIRST)
+        bias[item] = (1.0 - seen[:2 * TILES]) * HIDDEN
 
     def attend(item):
         origin = base[item] * TOKENS
@@ -248,12 +303,12 @@
 
                 @pl.when(here)
                 def _():
-                    pltpu.make_async_copy(source, o_out.at[item_heads[item]], o_recv).start()
+                    pltpu.make_async_copy(source, arrived.at[item_heads[item]], o_recv).start()
 
                 @pl.when(jnp.logical_not(here))
                 def _():
                     pltpu.make_async_remote_copy(
-                        src_ref=source, dst_ref=o_out.at[item_heads[item]],
+                        src_ref=source, dst_ref=arrived.at[item_heads[item]],
                         send_sem=o_send.at[item], recv_sem=o_recv,
                         device_id=(row * 4 + item_spans[item], tile), device_id_type=MESH,
                     ).start()
@@ -265,8 +320,34 @@
         def _():
             forward(which, 1).start()
 
-    start_major(1)
     start_major(2)
+
+    wait_item(1, 1)
+
+    @pl.when(fwd_major_sends)
+    def _():
+        forward(1, 0).start()
+
+    start_major(0)
+    wait_item(2, 1)
+
+    @pl.when(fwd_major_sends)
+    def _():
+        forward(2, 0).start()
+
+    start_shared(0)
+    for which in (1, 2, 0):
+        wait_item(which, 0)
+
+    @pl.when(jnp.logical_not(major_first))
+    def _():
+        for which in (1, 2):
+            ref = slot_ref(which, 0)
+            pltpu.make_async_copy(ref, ref, fwd_recv.at[which - 1, 0]).wait()
+
+    attend(0)
+    wait_item(0, 1)
+    attend(1)
     wait_item(0, 2)
 
     @pl.when(jnp.logical_not(shared_first))
@@ -277,35 +358,15 @@
 
     attend(2)
 
-    for which in (1, 2):
-        wait_item(which, 1)
-
-        @pl.when(fwd_major_sends)
-        def _():
-            forward(which, 0).start()
-
-    start_major(0)
-    for which in (1, 2, 0):
-        wait_item(which, 0)
-
-    @pl.when(jnp.logical_not(major_first))
-    def _():
-        for which in (1, 2):
-            ref = slot_ref(which, 0)
-            pltpu.make_async_copy(ref, ref, fwd_recv.at[which - 1, 0]).wait()
-
-    attend(0)
-    wait_item(0, 1)
-    attend(1)
-
-    pltpu.make_async_copy(o_out, o_out, o_recv).wait()
+    pltpu.make_async_copy(arrived, arrived, o_recv).wait()
+    o_out[...] = jnp.transpose(arrived[...], (1, 0, 2))
 
     for offset in range(1, 4):
         vis_block(offset).wait_send()
     for which in (0, 1, 2):
-        sent = ins[which].at[:31]
+        sent = ins.at[which, :31]
         pltpu.make_async_copy(sent, sent, in_send.at[which, 0]).wait()
-        sent = ins[which].at[:15]
+        sent = ins.at[which, :15]
         pltpu.make_async_copy(sent, sent, in_send.at[which, 1]).wait()
 
         @pl.when(jnp.logical_not(major_home))
@@ -327,30 +388,36 @@
             forward(which, 1).wait_send()
 
     for item in range(PER):
-        sent = o_out.at[:15]
+        sent = arrived.at[:15]
         pltpu.make_async_copy(sent, sent, o_send.at[item]).wait()
 
         @pl.when(item_spans[item] != local)
         def _():
-            last = o_out.at[0]
+            last = arrived.at[0]
             pltpu.make_async_copy(last, last, o_send.at[item]).wait()
 
 
-def exchange_and_attend(query, keys, values, visible):
+def per_device(query, keys, values, block_list, block_count):
     anywhere = pl.BlockSpec(memory_space=pl.ANY)
+    vmem = pl.BlockSpec(memory_space=pltpu.VMEM)
     return pl.pallas_call(
         kernel,
-        out_shape=jax.ShapeDtypeStruct((HEADS, TILE, WIDTH), jnp.bfloat16),
-        in_specs=[anywhere] * 4,
-        out_specs=anywhere,
+        out_shape=jax.ShapeDtypeStruct((TILE, HEADS, WIDTH), jnp.bfloat16),
+        in_specs=[anywhere, anywhere, anywhere, vmem, vmem],
+        out_specs=vmem,
         scratch_shapes=[
+            pltpu.VMEM((3, TILE, HEADS, WIDTH), jnp.bfloat16),
+            pltpu.VMEM((3, HEADS, TILE, WIDTH), jnp.bfloat16),
+            pltpu.VMEM((HEADS, TILE, WIDTH), jnp.bfloat16),
+            pltpu.VMEM((TILES, TILE), jnp.float32),
             pltpu.VMEM((PER * TOKENS, WIDTH), jnp.bfloat16),
             pltpu.VMEM((5 * TOKENS, WIDTH), jnp.bfloat16),
             pltpu.VMEM((WIDTH, 5 * TOKENS), jnp.bfloat16),
             pltpu.VMEM((PER, TOKENS, WIDTH), jnp.bfloat16),
-            pltpu.VMEM((4, 2 * TILES, TILE), jnp.float32),
+            pltpu.VMEM((4, TILES, TILE), jnp.float32),
             pltpu.VMEM((PER, 2 * TILES, TOKENS), jnp.float32),
             pltpu.VMEM((2 * TOKENS, QB), jnp.float32),
+            pltpu.SemaphoreType.DMA((3,)),
             pltpu.SemaphoreType.DMA((3, 2)),
             pltpu.SemaphoreType.DMA((3, PER)),
             pltpu.SemaphoreType.DMA,
@@ -361,30 +428,10 @@
             pltpu.SemaphoreType.DMA,
         ],
         compiler_params=pltpu.CompilerParams(
-            vmem_limit_bytes=56 << 20, has_side_effects=True
+            vmem_limit_bytes=56 << 20, has_side_effects=True, collective_id=0
         ),
         name="exchange_and_attend",
-    )(query, keys, values, visible)
-
-
-def visible_tiles(tile_lists, tile_counts):
-    slots = jnp.arange(2 * TILES, dtype=jnp.int32)
-    used = slots[None, :] < tile_counts[:, None]
-    named = (tile_lists[:, :, None] == slots[None, None, :]) & used[:, :, None]
-    return jnp.any(named, axis=1).T.astype(jnp.float32)
-
-
-def per_device(query, keys, values, block_list, block_count):
-    visible = jnp.pad(
-        visible_tiles(block_list[0], block_count[0]), ((0, 0), (0, TILE - TILES))
-    )
-    result = exchange_and_attend(
-        jnp.transpose(query[0], (1, 0, 2)),
-        jnp.transpose(keys[0], (1, 0, 2)),
-        jnp.transpose(values[0], (1, 2, 0)),
-        visible,
-    )
-    return jnp.transpose(result, (1, 0, 2))[None]
+    )(query[0], keys[0], values[0], block_list[0], block_count)[None]
 
 
 def solution(mesh):

time: 185 us -> 165 us (0.89)
  Pallas kernels: 172 us -> 162 us
  local copies, waits for them, and re-layouts: 9.3 us -> 2.65 us
  other arithmetic: 2.25 us -> 0 us
    pallas_call x1, Pallas kernels: 172 us -> 162 us  [per_device(): pl.pallas_call(kernel, out_shape=jax.ShapeDtypeStruct((TILE, HEADS, WIDTH...]
    broadcast_in_dim x1 -> x0, local copies, waits for them, and re-layouts: 3.57 us -> none  [per_device(): return jnp.transpose(result, (1, 0, 2))[None]]
    transpose x1 -> x0, local copies, waits for them, and re-layouts: 2.64 us -> none  [per_device(): jnp.transpose(keys[0], (1, 0, 2))]
where the time goes in v3:
time: 165 us
  Pallas kernels  162 us (98%)
  local copies, waits for them, and re-layouts  2.65 us (2%)
    pallas_call x1, Pallas kernels, per_device(): pl.pallas_call(kernel, out_shape=jax.ShapeDtypeStruct((TILE, HEADS, WIDTH...  162 us

profile of v3, /device:TPU:11, one launch (start us, length us, event | category | flops | bytes accessed | tf_op | source)
XLA Modules:
  0.0 164.6 jit_solution(9511547846893697072)
XLA Ops:
  0.0 161.9 %exchange_and_attend.1 = bf16[128,48,128]{2,1,0:T(8,128)(2,1)} custom-call(bf16[128,48,128]{2,1,0:T(8,128)(2,1)} %bitcast.6, bf16[128,48,128]{2,1,0:T(8,128)(2,1)} %bitcast.7, bf16[128,48,128]{2,1,0:T(8,128)(2,1)} %bitcast.8, s32[16,32]{1,0:T(8,128)} %bitcast.9, s32[1,16]{1,0:T(1,128)} %count_in.1), custom_call_target="tpu_custom_call" | custom-call | tf_op jit(solution)/shard_map/exchange_and_attend/pallas_call | solution.py:403
  161.9 2.7 %copy.7 = bf16[1,128,48,128]{3,2,1,0:T(8,128)(2,1)} copy(bf16[1,128,48,128]{3,2,1,0:T(8,128)(2,1)} %bitcast.5) | data formatting | bytes 3145728

commit v4 on v3

--- a/solution.py
+++ b/solution.py
@@ -17,8 +17,8 @@
 HEADS = 48
 PER = HEADS // SEQ
 WIDTH = 128
-QB = 512
-KB = 1024
+QB = 256
+KB = 256
 SCALE = math.log2(math.e) / math.sqrt(WIDTH)
 HIDDEN = -1e30
 CONTRACT_LAST = (((1,), (1,)), ((), ()))
@@ -46,7 +46,6 @@
     z = me_seq // 4 * 2 + plane
     me_group = x // 2 * 8 + z
     item_spans = (2 * core, 2 * core + 1, 2 * side + core)
-    item_heads = (3 * me_group + side, 3 * me_group + side, 3 * me_group + 2)
 
     base = (0, 1, 3)
 
@@ -253,64 +252,64 @@
         bias[item] = (1.0 - seen[:2 * TILES]) * HIDDEN
 
     def attend(item):
-        origin = base[item] * TOKENS
-
-        @pl.loop(0, TOKENS // QB)
-        def _(block):
-            start = pl.multiple_of(block * QB, QB)
-            columns = pl.ds(start, QB)
-            query = qb[pl.ds(pl.multiple_of(item * TOKENS + start, QB), QB), :]
-            chunks = TOKENS // KB + (block * QB + QB + KB - 1) // KB
-
-            def score(chunk, largest):
-                first = pl.multiple_of(chunk * KB, KB)
+        shared = item == 2
+        origin = pl.multiple_of(jnp.where(shared, 3, item) * TOKENS, TOKENS)
+        item_span = jnp.where(shared, 2 * side + core, 2 * core + item)
+        item_head = 3 * me_group + jnp.where(shared, 2, side)
+
+        def block_result(block):
+            columns = slice(block * QB, (block + 1) * QB)
+            query = qb[pl.ds(pl.multiple_of(item * TOKENS + block * QB, QB), QB), :]
+            held = scores.at[block % 2]
+            keys_seen = TOKENS + (block + 1) * QB
+
+            def hidden(tile):
+                return bias[item, tile:tile + 1, columns]
+
+            largest = jnp.full((8, QB), -3e38, jnp.float32)
+            for first in range(0, keys_seen, KB):
                 part = matmul(kb[pl.ds(origin + first, KB), :], query, CONTRACT_LAST)
-                scores[pl.ds(first, KB), :] = part
-                for tile in range(KB // TILE):
-                    rows = part[tile * TILE:(tile + 1) * TILE].reshape(TILE // 8, 8, QB)
-                    hidden = bias[item, pl.ds(chunk * (KB // TILE) + tile, 1), columns]
-                    largest = jnp.maximum(largest, jnp.max(rows, axis=0) + hidden)
-                return largest
-
-            largest = lax.fori_loop(0, chunks, score, jnp.full((8, QB), -3e38, jnp.float32))
+                held[first:first + KB, :] = part
+                for at in range(0, KB, TILE):
+                    rows = part[at:at + TILE].reshape(TILE // 8, 8, QB)
+                    largest = jnp.maximum(
+                        largest, jnp.max(rows, axis=0) + hidden((first + at) // TILE)
+                    )
             top = jnp.max(largest, axis=0, keepdims=True) * SCALE
 
-            def weigh(chunk, carry):
-                total, summed = carry
-                first = pl.multiple_of(chunk * KB, KB)
+            total = jnp.zeros((WIDTH, QB), jnp.float32)
+            summed = jnp.zeros((8, QB), jnp.float32)
+            for first in range(0, keys_seen, KB):
                 parts = []
-                for tile in range(KB // TILE):
-                    hidden = bias[item, pl.ds(chunk * (KB // TILE) + tile, 1), columns]
-                    rows = scores[pl.ds(first + tile * TILE, TILE), :]
-                    weight = jnp.exp2(rows * SCALE - (top - hidden))
+                for at in range(first, first + KB, TILE):
+                    weight = jnp.exp2(held[at:at + TILE, :] * SCALE - (top - hidden(at // TILE)))
                     summed = summed + jnp.sum(weight.reshape(TILE // 8, 8, QB), axis=0)
                     parts.append(weight.astype(jnp.bfloat16))
                 weights = jnp.concatenate(parts, 0)
-                total = total + matmul(vb[:, pl.ds(origin + first, KB)], weights, CONTRACT_PLAIN)
-                return total, summed
-
-            total, summed = lax.fori_loop(
-                0, chunks, weigh,
-                (jnp.zeros((WIDTH, QB), jnp.float32), jnp.zeros((8, QB), jnp.float32)),
-            )
+                total = total + matmul(
+                    vb[:, pl.ds(pl.multiple_of(origin + first, KB), KB)], weights, CONTRACT_PLAIN
+                )
             result = total / jnp.sum(summed, axis=0, keepdims=True)
             ob[item, columns, :] = jnp.transpose(result).astype(jnp.bfloat16)
 
-            for part in range(QB // TILE):
-                tile = block * (QB // TILE) + part
+        for block in range(TOKENS // QB):
+            block_result(block)
+
+            @pl.loop(block * (QB // TILE), (block + 1) * (QB // TILE))
+            def _(tile):
                 source = ob.at[item, pl.ds(pl.multiple_of(tile * TILE, TILE), TILE), :]
-                here = jnp.logical_and(item_spans[item] == local, tile == me_seq)
+                here = jnp.logical_and(item_span == local, tile == me_seq)
 
                 @pl.when(here)
                 def _():
-                    pltpu.make_async_copy(source, arrived.at[item_heads[item]], o_recv).start()
+                    pltpu.make_async_copy(source, arrived.at[item_head], o_recv).start()
 
                 @pl.when(jnp.logical_not(here))
                 def _():
                     pltpu.make_async_remote_copy(
-                        src_ref=source, dst_ref=arrived.at[item_heads[item]],
+                        src_ref=source, dst_ref=arrived.at[item_head],
                         send_sem=o_send.at[item], recv_sem=o_recv,
-                        device_id=(row * 4 + item_spans[item], tile), device_id_type=MESH,
+                        device_id=(row * 4 + item_span, tile), device_id_type=MESH,
                     ).start()
 
     for which in (1, 2):
@@ -345,18 +344,21 @@
             ref = slot_ref(which, 0)
             pltpu.make_async_copy(ref, ref, fwd_recv.at[which - 1, 0]).wait()
 
-    attend(0)
     wait_item(0, 1)
-    attend(1)
-    wait_item(0, 2)
-
-    @pl.when(jnp.logical_not(shared_first))
-    def _():
-        for which in (1, 2):
-            ref = slot_ref(which, 3)
-            pltpu.make_async_copy(ref, ref, fwd_recv.at[which - 1, 1]).wait()
-
-    attend(2)
+
+    @pl.loop(0, PER)
+    def _(item):
+        @pl.when(item == 2)
+        def _():
+            wait_item(0, 2)
+
+            @pl.when(jnp.logical_not(shared_first))
+            def _():
+                for which in (1, 2):
+                    ref = slot_ref(which, 3)
+                    pltpu.make_async_copy(ref, ref, fwd_recv.at[which - 1, 1]).wait()
+
+        attend(item)
 
     pltpu.make_async_copy(arrived, arrived, o_recv).wait()
     o_out[...] = jnp.transpose(arrived[...], (1, 0, 2))
@@ -416,7 +418,7 @@
             pltpu.VMEM((PER, TOKENS, WIDTH), jnp.bfloat16),
             pltpu.VMEM((4, TILES, TILE), jnp.float32),
             pltpu.VMEM((PER, 2 * TILES, TOKENS), jnp.float32),
-            pltpu.VMEM((2 * TOKENS, QB), jnp.float32),
+            pltpu.VMEM((2, 2 * TOKENS, QB), jnp.float32),
             pltpu.SemaphoreType.DMA((3,)),
             pltpu.SemaphoreType.DMA((3, 2)),
             pltpu.SemaphoreType.DMA((3, PER)),

time: 165 us -> 158 us (0.958)
  Pallas kernels: 162 us -> 156 us
    pallas_call x1, Pallas kernels: 162 us -> 156 us  [per_device(): pl.pallas_call(kernel, out_shape=jax.ShapeDtypeStruct((TILE, HEADS, WIDTH...]
where the time goes in v4:
time: 158 us
  Pallas kernels  156 us (99%)
  local copies, waits for them, and re-layouts  2.65 us (2%)
    pallas_call x1, Pallas kernels, per_device(): pl.pallas_call(kernel, out_shape=jax.ShapeDtypeStruct((TILE, HEADS, WIDTH...  156 us

profile of v4, /device:TPU:11, one launch (start us, length us, event | category | flops | bytes accessed | tf_op | source)
XLA Modules:
  0.0 158.2 jit_solution(2912845856040641327)
XLA Ops:
  0.0 155.6 %exchange_and_attend.1 = bf16[128,48,128]{2,1,0:T(8,128)(2,1)} custom-call(bf16[128,48,128]{2,1,0:T(8,128)(2,1)} %bitcast.6, bf16[128,48,128]{2,1,0:T(8,128)(2,1)} %bitcast.7, bf16[128,48,128]{2,1,0:T(8,128)(2,1)} %bitcast.8, s32[16,32]{1,0:T(8,128)} %bitcast.9, s32[1,16]{1,0:T(1,128)} %count_in.1), custom_call_target="tpu_custom_call" | custom-call | tf_op jit(solution)/shard_map/exchange_and_attend/pallas_call | solution.py:405
  155.6 2.7 %copy.7 = bf16[1,128,48,128]{3,2,1,0:T(8,128)(2,1)} copy(bf16[1,128,48,128]{3,2,1,0:T(8,128)(2,1)} %bitcast.5) | data formatting | bytes 3145728

commit v5 on v4

--- a/solution.py
+++ b/solution.py
@@ -31,8 +31,8 @@
 
 
 def kernel(
-    q_raw, k_raw, v_raw, list_in, count_in, o_out,
-    loaded, ins, arrived, vis_in, qb, kb, vb, ob, vis, bias, scores, load,
+    q_raw, k_raw, v_raw, list_in, count_in, arrived,
+    loaded, ins, vis_in, qb, kb, vb, ob, vis, bias, scores, load,
     in_send, in_recv, vis_send, vis_recv, fwd_send, fwd_recv, o_send, o_recv,
 ):
     me_span = lax.axis_index("span")
@@ -68,6 +68,12 @@
     def item_slot(which, item):
         return item if which == 0 else base[item] + 1
 
+    def group_at(step):
+        turn = step // 2
+        far = (turn + 1) // 2
+        z_step = (lax.rem(turn, 2) * 2 * far - far) * (1 - 2 * side)
+        return lax.rem(x // 2 + step, 2) * 8 + lax.rem(z + z_step + 8, 8)
+
     def chip(group, x_side, its_core):
         its_z = lax.rem(group, 8)
         return (
@@ -76,7 +82,7 @@
         )
 
     def major_block(which, step, x_side):
-        group = lax.rem(me_group + step, 16)
+        group = group_at(step)
         item = lax.rem(local, 2)
         slot = item if which == 0 else 1 + item
         return pltpu.make_async_remote_copy(
@@ -87,7 +93,7 @@
         )
 
     def shared_block(which, step):
-        group = lax.rem(me_group + step, 16)
+        group = group_at(step)
         return pltpu.make_async_remote_copy(
             src_ref=ins.at[which, 3 * group + 2],
             dst_ref=place(which, item_slot(which, 2), me_seq),
@@ -361,7 +367,6 @@
         attend(item)
 
     pltpu.make_async_copy(arrived, arrived, o_recv).wait()
-    o_out[...] = jnp.transpose(arrived[...], (1, 0, 2))
 
     for offset in range(1, 4):
         vis_block(offset).wait_send()
@@ -399,18 +404,21 @@
             pltpu.make_async_copy(last, last, o_send.at[item]).wait()
 
 
+def by_token(by_head, out):
+    out[...] = jnp.transpose(by_head[...], (1, 0, 2))
+
+
 def per_device(query, keys, values, block_list, block_count):
     anywhere = pl.BlockSpec(memory_space=pl.ANY)
     vmem = pl.BlockSpec(memory_space=pltpu.VMEM)
-    return pl.pallas_call(
+    by_head = pl.pallas_call(
         kernel,
-        out_shape=jax.ShapeDtypeStruct((TILE, HEADS, WIDTH), jnp.bfloat16),
+        out_shape=jax.ShapeDtypeStruct((HEADS, TILE, WIDTH), jnp.bfloat16),
         in_specs=[anywhere, anywhere, anywhere, vmem, vmem],
-        out_specs=vmem,
+        out_specs=anywhere,
         scratch_shapes=[
             pltpu.VMEM((3, TILE, HEADS, WIDTH), jnp.bfloat16),
             pltpu.VMEM((3, HEADS, TILE, WIDTH), jnp.bfloat16),
-            pltpu.VMEM((HEADS, TILE, WIDTH), jnp.bfloat16),
             pltpu.VMEM((TILES, TILE), jnp.float32),
             pltpu.VMEM((PER * TOKENS, WIDTH), jnp.bfloat16),
             pltpu.VMEM((5 * TOKENS, WIDTH), jnp.bfloat16),
@@ -433,7 +441,16 @@
             vmem_limit_bytes=56 << 20, has_side_effects=True, collective_id=0
         ),
         name="exchange_and_attend",
-    )(query[0], keys[0], values[0], block_list[0], block_count)[None]
+    )(query[0], keys[0], values[0], block_list[0], block_count)
+    rows = TILE // 2
+    return pl.pallas_call(
+        by_token,
+        grid=(2,),
+        out_shape=jax.ShapeDtypeStruct((TILE, HEADS, WIDTH), jnp.bfloat16),
+        in_specs=[pl.BlockSpec((HEADS, rows, WIDTH), lambda i: (0, i, 0))],
+        out_specs=pl.BlockSpec((rows, HEADS, WIDTH), lambda i: (i, 0, 0)),
+        name="by_token",
+    )(by_head)[None]
 
 
 def solution(mesh):

time: 158 us -> 156 us (0.987); the launches traced: 158 us -> 154 us
  local copies, waits for them, and re-layouts: 2.65 us -> 0 us
  Pallas kernels: 156 us -> 154 us
    unnamed x1 -> x0, local copies, waits for them, and re-layouts: 2.65 us -> none
    pallas_call x1 -> x2, Pallas kernels: 156 us -> 154 us  [the longest x1 152 us: per_device(): pl.pallas_call(kernel, out_shape=jax.ShapeDtypeStruct((HEADS, TILE, WIDTH...]
where the time goes in v5:
time: 156 us; the launch traced here: 154 us
  Pallas kernels  154 us (99%)
    pallas_call x1, Pallas kernels, per_device(): pl.pallas_call(kernel, out_shape=jax.ShapeDtypeStruct((HEADS, TILE, WIDTH...  152 us

profile of v5, /device:TPU:11, one launch (start us, length us, event | category | flops | bytes accessed | tf_op | source)
XLA Modules:
  0.0 154.3 jit_solution(11996354996350351574)
XLA Ops:
  0.0 151.8 %exchange_and_attend.1.by_head = bf16[48,128,128]{2,1,0:T(8,128)(2,1)} custom-call(bf16[128,48,128]{2,1,0:T(8,128)(2,1)} %bitcast.5, bf16[128,48,128]{2,1,0:T(8,128)(2,1)} %bitcast.6, bf16[128,48,128]{2,1,0:T(8,128)(2,1)} %bitcast.7, s32[16,32]{1,0:T(8,128)} %bitcast.8, s32[1,16]{1,0:T(1,128)} %count_in.1), custom_call_target="tpu_custom_call" | custom-call | tf_op jit(solution)/shard_map/exchange_and_attend/pallas_call | solution.py:414
  151.9 2.5 %by_token.1 = bf16[128,48,128]{2,1,0:T(8,128)(2,1)} custom-call(bf16[48,128,128]{2,1,0:T(8,128)(2,1)} %exchange_and_attend.1.by_head), custom_call_target="tpu_custom_call" | custom-call | tf_op jit(solution)/shard_map/by_token/pallas_call | solution.py:446

commit v6 on v5

--- a/solution.py
+++ b/solution.py
@@ -123,9 +123,9 @@
         major_block(which, 0, 1 - side).start()
 
         @pl.loop(1, 16)
-        def _(step):
-            major_block(which, step, side).start()
-            major_block(which, step, 1 - side).start()
+        def _(near):
+            major_block(which, 16 - near, side).start()
+            major_block(which, 16 - near, 1 - side).start()
 
     def start_shared(which):
         @pl.when(shared_home)
@@ -141,8 +141,8 @@
             shared_block(which, 0).start()
 
         @pl.loop(1, 16)
-        def _(step):
-            shared_block(which, step).start()
+        def _(near):
+            shared_block(which, 16 - near).start()
 
     def wait_item(which, item):
         ref = slot_ref(which, item_slot(which, item))

time: 156 us -> 156 us (level); the launches traced: 154 us -> 156 us
  Pallas kernels: 154 us -> 156 us
    pallas_call x1, Pallas kernels: 152 us -> 153 us  [per_device(): pl.pallas_call(kernel, out_shape=jax.ShapeDtypeStruct((HEADS, TILE, WIDTH...]
where the time goes in v6:
time: 156 us
  Pallas kernels  156 us (100%)
    pallas_call x1, Pallas kernels, per_device(): pl.pallas_call(kernel, out_shape=jax.ShapeDtypeStruct((HEADS, TILE, WIDTH...  153 us

profile of v6, /device:TPU:11, one launch (start us, length us, event | category | flops | bytes accessed | tf_op | source)
XLA Modules:
  0.0 156.0 jit_solution(2147987424469575261)
XLA Ops:
  0.0 153.5 %exchange_and_attend.1.by_head = bf16[48,128,128]{2,1,0:T(8,128)(2,1)} custom-call(bf16[128,48,128]{2,1,0:T(8,128)(2,1)} %bitcast.5, bf16[128,48,128]{2,1,0:T(8,128)(2,1)} %bitcast.6, bf16[128,48,128]{2,1,0:T(8,128)(2,1)} %bitcast.7, s32[16,32]{1,0:T(8,128)} %bitcast.8, s32[1,16]{1,0:T(1,128)} %count_in.1), custom_call_target="tpu_custom_call" | custom-call | tf_op jit(solution)/shard_map/exchange_and_attend/pallas_call | solution.py:414
  153.5 2.5 %by_token.1 = bf16[128,48,128]{2,1,0:T(8,128)(2,1)} custom-call(bf16[48,128,128]{2,1,0:T(8,128)(2,1)} %exchange_and_attend.1.by_head), custom_call_target="tpu_custom_call" | custom-call | tf_op jit(solution)/shard_map/by_token/pallas_call | solution.py:446
